TPU v7x, 32 devices: a whole 2x2x4 slice. The times are simulated.
32 devices in a mesh: leaf: 8 (over z, x), vec: 4 (over y, core).
Axes of the slice: x: 2, y: 2, z: 4, core: 2. Of those that a mesh axis runs over, the one named last changes fastest.
Arguments:
- panels: float32 [32, 65536], P('vec', 'leaf'), may hold values from -6 to 6
- near_tiles: float32 [512, 4, 128, 128], P('leaf', None, 'vec'), may hold values from -0.25 to 0.25
- near_cols: int32 [512, 4], P('leaf'), may hold values from 0 to 511, as said below
- leaf_order: int32 [512, 128], P('leaf'), may hold values from 0 to 127, each once within a row
- leaf_basis: float32 [512, 64, 128], P('leaf'), may hold values from -0.5 to 0.5
- local_mats: float32 [8, 63, 64, 128], P('leaf'), may hold values from -0.75 to 0.75
- local_flags: int32 [8, 63], P('leaf'), may hold values 0 or 1
- cross_coupling: float32 [6, 64, 64], replicated, may hold values from -0.75 to 0.75
- cross_transfer: float32 [4, 64, 64], replicated, may hold values from -0.75 to 0.75
- cross_flags: int32 [6], replicated, may hold values 0 or 1
Outputs:
- product: float32 [32, 65536], P('vec', 'leaf')
Inputs may be any that keep to these rules, and one draw needn't show every extreme that they name: `near_cols`: every entry of row i names a leaf within 8 leaves of leaf i. `leaf_order`: each row is a permutation of 0 to 127.
All inputs are finite; a program needn't handle non-finite values. No bound on the sum of `local_flags` on one device may be relied on, other than what follows from the above.
Results may differ from a plain program's by a relative error of at most 0.00022.
Values sent between devices are 32-bit elements; how exact they have to be, the bound alone decides.
A program may use at most 64 MiB of HBM per device.

v0:
```python
import math
import jax
import jax.numpy as jnp
from jax import lax
from jax.sharding import PartitionSpec as P

W = 8
precise = lax.Precision.HIGHEST
root_half = 1.0 / math.sqrt(2.0)


def extended_2(cells, sides, width):
    for axis, dim in sides:
        count = lax.axis_size(axis)
        ends = count - 1
        head = lax.slice_in_dim(cells, 0, width, axis=dim)
        tail = lax.slice_in_dim(cells, cells.shape[dim] - width, cells.shape[dim], axis=dim)
        cells = jnp.concatenate(
            [
                lax.ppermute(tail, axis, [(i, (i + 1) % count) for i in range(ends)]),
                cells,
                lax.ppermute(head, axis, [((i + 1) % count, i) for i in range(ends)]),
            ],
            axis=dim,
        )
    return cells


def partner(block, axis, bit):
    count = lax.axis_size(axis)
    route = []
    for low in range(count):
        high = low | 1 << bit
        if high != low and high < count:
            route += [(low, high), (high, low)]
    return lax.ppermute(block, axis, route)


def near_product(tile_rows, sources):
    return jnp.einsum("lnqp,slnp->slq", tile_rows, sources, precision=precise)


def local(
    panels,
    near_tiles,
    near_cols,
    leaf_order,
    leaf_basis,
    local_mats,
    local_flags,
    cross_coupling,
    cross_transfer,
    cross_flags,
):
    rhs_dev = panels.shape[0]
    leaves = leaf_basis.shape[0]
    skel_rank = leaf_basis.shape[1]
    leaf_size = leaf_basis.shape[2]
    halo_cells = W * leaf_size
    leaf_count = lax.axis_size("leaf")
    leaf_index = lax.axis_index("leaf")
    cross_depth = leaf_count.bit_length() - 1
    places = jnp.arange(leaf_size, dtype=jnp.int32)
    order_hot = (leaf_order[:, :, None] == places[None, None, :]).astype(jnp.float32)
    ordered = jnp.einsum(
        "lpm,slm->slp", order_hot, panels.reshape(rhs_dev, leaves, leaf_size), precision=precise
    )
    ordered_flat = ordered.reshape(rhs_dev, leaves * leaf_size)
    local_cols = near_cols - leaf_index * leaves + W
    rim_leaves = jnp.arange(leaves + 2 * W, dtype=jnp.int32)
    select_hot = (local_cols[:, :, None] == rim_leaves[None, None, :]).astype(jnp.float32)
    gathered = lax.all_gather(ordered_flat, "vec", axis=0, tiled=True)
    extended = extended_2(gathered, (("leaf", 1),), halo_cells)
    blocked = extended.reshape(extended.shape[0], leaves + 2 * W, leaf_size)
    partial_rows = near_product(
        near_tiles, jnp.einsum("lne,sep->slnp", select_hot, blocked, precision=precise)
    )
    near_field = lax.all_to_all(partial_rows, "vec", split_axis=0, concat_axis=2, tiled=True)
    local_blocks = local_mats[0]
    local_admit = local_flags[0].astype(jnp.float32)
    leaf_skel = jnp.einsum("lkp,slp->lsk", leaf_basis, ordered, precision=precise)
    skeleton = leaf_skel.reshape(leaves // 2, 2, rhs_dev, skel_rank).sum(axis=1) * root_half
    local_depth = leaves.bit_length() - 1
    coupled = []
    for tree_level in range(1, local_depth):
        node_count = leaves >> tree_level
        first_node = leaves - (leaves >> tree_level - 1)
        blocks = local_blocks[first_node : first_node + node_count]
        sibling = skeleton.reshape(node_count // 2, 2, rhs_dev, skel_rank)[:, ::-1].reshape(
            skeleton.shape
        )
        term = jnp.einsum("jkm,jsm->jsk", blocks[:, :, :skel_rank], sibling, precision=precise)
        coupled.append(local_admit[first_node : first_node + node_count, None, None] * term)
        lifted = jnp.einsum("jsk,jkm->jsm", skeleton, blocks[:, :, skel_rank:], precision=precise)
        skeleton = lifted.reshape(node_count // 2, 2, rhs_dev, skel_rank).sum(axis=1) * root_half
    device_block = local_blocks[leaves - 2]
    device_skel = skeleton[0]
    device_lift = jnp.dot(device_skel, device_block[:, skel_rank:], precision=precise)

    def cross_index(level_bit):
        return leaf_count - (leaf_count >> level_bit - 1) + (leaf_index >> level_bit)

    def transfer_at(level_bit):
        if level_bit == 0:
            return device_block[:, skel_rank:]
        return lax.dynamic_index_in_dim(cross_transfer, cross_index(level_bit), 0, keepdims=False)

    cross_terms = []
    current, carried = (device_skel, device_lift)
    for level_bit in range(cross_depth):
        sibling_skel, sibling_up = partner((current, carried), "leaf", level_bit)
        if level_bit == 0:
            coupling = device_block[:, :skel_rank]
            admitted = local_admit[leaves - 2]
        else:
            node_index = cross_index(level_bit)
            coupling = lax.dynamic_index_in_dim(cross_coupling, node_index, 0, keepdims=False)
            admitted = lax.dynamic_index_in_dim(cross_flags, node_index, 0, keepdims=False).astype(
                jnp.float32
            )
        cross_terms.append(admitted * jnp.dot(sibling_skel, coupling.T, precision=precise))
        if level_bit < cross_depth - 1:
            current = (carried + sibling_up) * root_half
            if level_bit + 1 <= cross_depth - 2:
                carried = jnp.dot(current, transfer_at(level_bit + 1), precision=precise)
    downward = cross_terms[cross_depth - 1]
    for level_bit in range(cross_depth - 2, -1, -1):
        downward = cross_terms[level_bit] + jnp.dot(
            downward, transfer_at(level_bit).T, precision=precise
        )
    downward = downward[None]
    for tree_level in range(local_depth - 1, 0, -1):
        node_count = leaves >> tree_level
        first_node = leaves - (leaves >> tree_level - 1)
        transfer = local_blocks[first_node : first_node + node_count, :, skel_rank:]
        spread = jnp.repeat(downward, 2, axis=0)
        downward = coupled[tree_level - 1] + jnp.einsum(
            "jkm,jsm->jsk", transfer, spread, precision=precise
        )
    far_field = jnp.einsum(
        "lkp,lsk->slp", leaf_basis, jnp.repeat(downward, 2, axis=0), precision=precise
    )
    combined = near_field + far_field
    restored = jnp.einsum("lpm,slp->slm", order_hot, combined, precision=precise)
    return restored.reshape(rhs_dev, leaves * leaf_size)


def solution(mesh):
    return jax.shard_map(
        local,
        mesh=mesh,
        in_specs=(
            P("vec", "leaf"),
            P("leaf", None, "vec", None),
            P("leaf", None),
            P("leaf", None),
            P("leaf", None, None),
            P("leaf", None, None, None),
            P("leaf", None),
            P(),
            P(),
            P(),
        ),
        out_specs=P("vec", "leaf"),
        check_vma=False,
    )
```

profile of v0, /device:TPU:0, one launch (start us, length us, event | category | flops | bytes accessed | tf_op | source)
XLA Modules:
  0.0 107.7 jit_solution(1029454340300619483)
XLA Ops:
  6.5 1.4 %slice_bitcast_fusion = f32[32,64,128]{2,1,0:T(8,128)S(1)} fusion(f32[1,63,64,128]{3,2,1,0:T(8,128)} %param.15), kind=kLoop, calls=%fused_computation.34 | loop fusion | bytes 2097152 | tf_op jit(solution)/shard_map/slice | solution.py:88
  8.0 1.1 %slice_bitcast_fusion.1 = f32[16,64,128]{2,1,0:T(8,128)S(1)} fusion(f32[1,63,64,128]{3,2,1,0:T(8,128)} %param.15), kind=kLoop, calls=%fused_computation.39 | loop fusion | bytes 1048576 | tf_op jit(solution)/shard_map/slice | solution.py:88
  9.1 1.2 %slice_bitcast_fusion.2 = f32[8,64,128]{2,1,0:T(8,128)S(1)} fusion(f32[1,63,64,128]{3,2,1,0:T(8,128)} %param.15), kind=kLoop, calls=%fused_computation.48 | loop fusion | bytes 524288 | tf_op jit(solution)/shard_map/slice | solution.py:88
  10.3 0.9 slice_bitcast_fusion.3
  11.2 0.9 slice_bitcast_fusion.4
  12.1 4.7 %fusion.2 = f32[64,128,8]{1,2,0:T(8,128)S(1)} fusion(s32[64,128]{1,0:T(8,128)S(1)} %copy-done.18, f32[8,8192]{1,0:T(8,128)S(1)} %copy-done.17), kind=kOutput, calls=%fused_computation.4 | convolution fusion | flops 101711872 | bytes 557056 | tf_op jit(solution)/shard_map/lpm,slm->slp/dot_general | solution.py:65
  16.9 3.4 %bitcast_reduce_fusion = f32[32,8,64]{2,1,0:T(8,128)S(1)} fusion(f32[64,64,128]{2,1,0:T(8,128)S(1)} %copy-done, f32[64,128,8]{1,2,0:T(8,128)S(1)} %fusion.2), kind=kOutput, calls=%fused_computation.44 | convolution fusion | flops 50348032 | bytes 2424832 | tf_op jit(solution)/shard_map/lkp,slp->lsk/dot_general | solution.py:81
  20.2 1.2 %bitcast_reduce_fusion.1 = f32[16,8,64]{2,1,0:T(8,128)S(1)} fusion(f32[32,64,128]{2,1,0:T(8,128)S(1)} %slice_bitcast_fusion, f32[32,8,64]{2,1,0:T(8,128)S(1)} %bitcast_reduce_fusion), kind=kOutput, calls=%fused_computation.53 | convolution fusion | flops 12607488 | bytes 1146880 | tf_op jit(solution)/shard_map/jsk,jkm->jsm/dot_general | solution.py:94
  21.4 0.7 bitcast_reduce_fusion.2
  22.8 0.8 fusion.12
  23.7 3.0 %collective-permute-start.2 = (f32[8,64]{1,0:T(8,128)}, f32[8,64]{1,0:T(8,128)}, u32[]{:S(2)}, u32[]{:S(2)}) collective-permute-start(f32[8,64]{1,0:T(8,128)} %fusion.12), channel_id=1, source_target_pairs={{0,4},{4,0},{8,12},{12,8},{16,20},{20,16},{24,28},{28,24},{1,5},{5... | collective-permute-start | bytes 6152 | tf_op jit(solution)/shard_map/ppermute | solution.py:36
  26.6 0.8 slice_bitcast_fusion.5
  28.0 1.5 %fusion.68 = f32[8,64]{1,0:T(8,128)} fusion(f32[8,64]{1,0:T(8,128)} %fusion.12, f32[64,128]{1,0:T(8,128)S(1)} %slice_bitcast_fusion.5), kind=kOutput, calls=%fused_computation.84 | convolution fusion | flops 393216 | bytes 36864 | tf_op jit(solution)/shard_map/dot_general | solution.py:98
  29.5 0.7 convert_element_type.18
  30.4 0.8 reverse_multiply_fusion.2
  31.2 0.8 reverse_multiply_fusion.1
  32.1 1.9 %convolution_multiply_fusion.3 = f32[4,8,64]{2,1,0:T(8,128)} fusion(f32[4,8,64]{2,1,0:T(8,128)S(1)} %bitcast.147, f32[4,64,128]{2,1,0:T(8,128)} %copy-done.4, f32[4]{0:T(128)S(1)} %slice_bitcast_fusion.7), kind=kOutput, calls=%fused_computation.20 | convolution fusion | flops 1574912 | bytes 147472 | tf_op jit(solution)/shard_map/jkm,jsm->jsk/dot_general | solution.py:92
  34.5 2.0 %convolution_multiply_fusion.1 = f32[16,8,64]{2,1,0:T(8,128)S(1)} fusion(f32[16,8,64]{2,1,0:T(8,128)S(1)} %bitcast.142, f32[16,64,128]{2,1,0:T(8,128)} %copy-done.1, f32[16]{0:T(128)S(1)} %slice_bitcast_fusion.9), kind=kOutput, calls=%fused_computation.16 | convolution fusion | flops 6299648 | bytes 589888 | tf_op jit(solution)/shard_map/jkm,jsm->jsk/dot_general | solution.py:92
  36.5 1.8 %convolution_multiply_fusion = f32[32,8,64]{2,1,0:T(8,128)S(1)} fusion(f32[32,8,64]{2,1,0:T(8,128)S(1)} %bitcast.139, f32[32,64,128]{2,1,0:T(8,128)S(1)} %slice_bitcast_fusion, f32[32]{0:T(128)S(1)} %slice_bitcast_fusion.10), kind=kOutput, calls=%fused_computation.14 | convolution fusion | flops 12599296 | bytes 1179776 | tf_op jit(solution)/shard_map/jkm,jsm->jsk/dot_general | solution.py:92
  38.3 0.7 add_multiply_fusion.1
  39.0 0.9 fusion.55
  39.9 2.1 %collective-permute-start.5 = (f32[8,64]{1,0:T(8,128)S(1)}, f32[8,64]{1,0:T(8,128)S(1)}, u32[]{:S(2)}, u32[]{:S(2)}) collective-permute-start(f32[8,64]{1,0:T(8,128)S(1)} %fusion.55), channel_id=1, source_target_pairs={{0,8},{8,0},{4,12},{12,4},{16,24},{24,16},{20,28},{28,20},{1,9},{9... | collective-permute-start | bytes 6152 | tf_op jit(solution)/shard_map/ppermute | solution.py:36
  42.2 1.4 %collective-permute-done.5 = f32[8,64]{1,0:T(8,128)S(1)} collective-permute-done((f32[8,64]{1,0:T(8,128)S(1)}, f32[8,64]{1,0:T(8,128)S(1)}, u32[]{:S(2)}, u32[]{:S(2)}) %collective-permute-start.5) | collective-permute-done | bytes 2080 | tf_op jit(solution)/shard_map/ppermute | solution.py:36
  43.6 3.0 %collective-permute-start.6 = (f32[8,64]{1,0:T(8,128)S(1)}, f32[8,64]{1,0:T(8,128)S(1)}, u32[]{:S(2)}, u32[]{:S(2)}) collective-permute-start(f32[8,64]{1,0:T(8,128)S(1)} %add_multiply_fusion), channel_id=1, source_target_pairs={{0,16},{16,0},{4,20},{20,4},{8,24},{24,8},{12,28},{28,12},{1,17},{... | collective-permute-start | bytes 6152 | tf_op jit(solution)/shard_map/ppermute | solution.py:36
  46.6 1.2 %slice.157 = f32[1,1]{1,0:T(1,128)} slice(f32[1,63]{1,0:T(1,128)} %copy-done.20), slice={[0:1], [62:63]} | slice | bytes 8 | tf_op jit(solution)/shard_map/slice | solution.py:114
  49.8 1.6 %collective-permute-start.4 = (f32[8,64]{1,0:T(8,128)S(1)}, f32[8,64]{1,0:T(8,128)S(1)}, u32[]{:S(2)}, u32[]{:S(2)}) collective-permute-start(f32[8,64]{1,0:T(8,128)S(1)} %add_multiply_fusion.1), channel_id=1, source_target_pairs={{0,8},{8,0},{4,12},{12,4},{16,24},{24,16},{20,28},{28,20},{1,9},{9... | collective-permute-start | bytes 6152 | tf_op jit(solution)/shard_map/ppermute | solution.py:36
  51.4 0.9 convolution_multiply_fusion.5
  52.3 0.9 fusion.53
  53.4 0.9 fusion.10
  54.6 1.4 %fusion.11 = f32[8,64]{1,0:T(8,128)S(1)} fusion(f32[8,64]{1,0:T(8,128)S(1)} %fusion.66, f32[8,64]{1,0:T(8,128)} %collective-permute-done.2, f32[64,128]{1,0:T(8,128)S(1)} %copy-done.10, f32[]{:T(128)} %bitcast.35), kind=kOutput, calls=%fused_computation.27 | convolution fusion | flops 394240 | bytes 38916 | tf_op jit(solution)/shard_map/dot_general | solution.py:121
  56.0 1.1 %convolution_add_fusion.4 = f32[2,8,64]{2,1,0:T(8,128)S(1)} fusion(f32[2,8,64]{2,1,0:T(8,128)S(1)} %convolution_multiply_fusion.4, f32[63,64,128]{2,1,0:T(8,128)} %bitcast.126, f32[8,64]{1,0:T(8,128)S(1)} %fusion.11), kind=kOutput, calls=%fused_computation.21 | convolution fusion | flops 787456 | bytes 75776 | tf_op jit(solution)/shard_map/jkm,jsm->jsk/dot_general | solution.py:137
  57.1 1.3 %convolution_add_fusion.3 = f32[4,8,64]{2,1,0:T(8,128)S(1)} fusion(f32[4,8,64]{2,1,0:T(8,128)S(1)} %copy-done.14, f32[4,8,64]{2,1,0:T(8,128)S(1)} %bitcast.148, f32[63,64,128]{2,1,0:T(8,128)} %bitcast.127), kind=kOutput, calls=%fused_computation.19 | convolution fusion | flops 1574912 | bytes 155648 | tf_op jit(solution)/shard_map/jkm,jsm->jsk/dot_general | solution.py:137
  58.5 1.5 %convolution_add_fusion.2 = f32[8,8,64]{2,1,0:T(8,128)S(1)} fusion(f32[8,8,64]{2,1,0:T(8,128)S(1)} %convolution_multiply_fusion.2, f32[8,8,64]{2,1,0:T(8,128)S(1)} %bitcast.146, f32[63,64,128]{2,1,0:T(8,128)} %bitcast.128), kind=kOutput, calls=%fused_computation.17 | convolution fusion | flops 3149824 | bytes 311296 | tf_op jit(solution)/shard_map/jkm,jsm->jsk/dot_general | solution.py:137
  60.0 1.1 fusion.94
  61.1 3.4 %collective-permute-start = (f32[32,1024]{1,0:T(8,128)S(1)}, f32[32,1024]{1,0:T(8,128)S(1)}, u32[]{:S(2)}, u32[]{:S(2)}) collective-permute-start(f32[32,1024]{1,0:T(8,128)S(1)} %get-tuple-element.5), channel_id=1, source_target_pairs={{0,4},{4,8},{8,12},{12,16},{16,20},{20,24},{24,28},{1,5},{5,9},{9,... | collective-permute-start | bytes 393224 | tf_op jit(solution)/shard_map/ppermute | solution.py:20
  64.5 1.5 %collective-permute-start.1 = (f32[32,1024]{1,0:T(8,128)S(1)}, f32[32,1024]{1,0:T(8,128)S(1)}, u32[]{:S(2)}, u32[]{:S(2)}) collective-permute-start(f32[32,1024]{1,0:T(8,128)S(1)} %get-tuple-element.6), channel_id=1, source_target_pairs={{4,0},{8,4},{12,8},{16,12},{20,16},{24,20},{28,24},{5,1},{9,5},{13... | collective-permute-start | bytes 393224 | tf_op jit(solution)/shard_map/ppermute | solution.py:22
  66.0 2.0 %convolution_add_fusion.1 = f32[16,8,64]{2,1,0:T(8,128)S(1)} fusion(f32[16,8,64]{2,1,0:T(8,128)S(1)} %convolution_multiply_fusion.1, f32[16,8,64]{2,1,0:T(8,128)S(1)} %bitcast.143, f32[63,64,128]{2,1,0:T(8,128)} %bitcast.129), kind=kOutput, calls=%fused_computation.15 | convolution fusion | flops 6299648 | bytes 622592 | tf_op jit(solution)/shard_map/jkm,jsm->jsk/dot_general | solution.py:137
  68.4 3.0 %collective-permute-done.1 = f32[32,1024]{1,0:T(8,128)S(1)} collective-permute-done((f32[32,1024]{1,0:T(8,128)S(1)}, f32[32,1024]{1,0:T(8,128)S(1)}, u32[]{:S(2)}, u32[]{:S(2)}) %collective-permute-start.1) | collective-permute-done | bytes 131104 | tf_op jit(solution)/shard_map/ppermute | solution.py:22
  71.7 1.9 %convolution_bitcast_fusion.1 = f32[32,64,4,128]{3,1,2,0:T(8,128)S(1)} fusion(f32[32,80,128,1]{2,1,0,3:T(8,128)S(1)} %bitcast.131, s32[64,4]{0,1:T(4,128)S(1)} %subtract_add_fusion), kind=kOutput, calls=%fused_computation.5 | convolution fusion | flops 1006653440 | bytes 5506048 | tf_op jit(solution)/shard_map/lne,sep->slnp/dot_general | solution.py:76
  73.9 6.2 %fusion.5 = f32[32,64,32]{2,0,1:T(8,128)S(1)} fusion(f32[64,4,32,128]{3,2,1,0:T(8,128)S(1)} %copy-done.2, f32[32,64,4,128]{3,1,2,0:T(8,128)S(1)} %convolution_bitcast_fusion.1), kind=kOutput, calls=%fused_computation.8 | convolution fusion | flops 402653184 | bytes 8650752 | tf_op jit(solution)/shard_map/lnqp,slnp->slq/dot_general | solution.py:40
  80.1 1.4 %copy.17 = f32[32,64,32]{1,2,0:T(8,128)} copy(f32[32,64,32]{2,0,1:T(8,128)S(1)} %fusion.5) | data formatting | bytes 524288 | tf_op jit(solution)/shard_map/lnqp,slnp->slq/transpose | solution.py:40
  81.5 2.1 %reshape.130 = f32[4,1,16384]{2,1,0:T(1,128)} reshape(f32[32,32,64]{2,1,0:T(8,128)} %bitcast.132) | data formatting | bytes 524288
  83.6 3.6 %all-to-all-start = ((f32[4,1,16384]{2,1,0:T(1,128)}), f32[4,1,16384]{2,1,0:T(1,128)S(1)}, u32[]{:S(2)}, u32[]{:S(2)}) async-start(f32[4,1,16384]{2,1,0:T(1,128)} %reshape.130), calls=%async_computation | async-start | bytes 524288 | tf_op jit(solution)/shard_map/all_to_all | solution.py:78
  87.2 3.0 %convolution_add_fusion = f32[32,8,64]{2,1,0:T(8,128)S(1)} fusion(f32[32,8,64]{2,1,0:T(8,128)S(1)} %convolution_multiply_fusion, f32[32,8,64]{2,1,0:T(8,128)S(1)} %bitcast.140, f32[63,64,128]{2,1,0:T(8,128)} %bitcast.130), kind=kOutput, calls=%fused_computation.13 | convolution fusion | flops 12599296 | bytes 1245184 | tf_op jit(solution)/shard_map/jkm,jsm->jsk/dot_general | solution.py:137
  90.3 2.7 %all-to-all-done = f32[4,1,16384]{2,1,0:T(1,128)S(1)} async-done(((f32[4,1,16384]{2,1,0:T(1,128)}), f32[4,1,16384]{2,1,0:T(1,128)S(1)}, u32[]{:S(2)}, u32[]{:S(2)}) %all-to-all-start) | async-done | bytes 262176 | tf_op jit(solution)/shard_map/all_to_all | solution.py:78
  93.5 1.4 %reduce.2 = f32[4,16384]{1,0:T(4,128)S(1)} reduce(f32[4,1,16384]{2,1,0:T(1,128)S(1)} %all-to-all-done, f32[]{:T(128)} %broadcast.17), dimensions={1}, to_apply=%all_to_all.13.reduce_sub_computation | reduce | bytes 524292 | tf_op jit(solution)/shard_map/all_to_all | solution.py:78
  95.4 1.9 %fusion.9 = f32[8,64,128]{2,0,1:T(8,128)S(1)} fusion(f32[8,64,128]{2,0,1:T(8,128)S(1)} %copy.19, f32[64,8,64]{2,1,0:T(8,128)S(1)} %bitcast.137, f32[64,64,128]{2,1,0:T(8,128)S(1)} %copy-done), kind=kOutput, calls=%fused_computation.12 | convolution fusion | flops 50397184 | bytes 2752512 | tf_op jit(solution)/shard_map/lkp,lsk->slp/dot_general | solution.py:140
  97.3 3.6 %convolution_bitcast_fusion = f32[8,8192]{1,0:T(8,128)} fusion(f32[8,64,128]{2,0,1:T(8,128)S(1)} %fusion.9, s32[64,128]{1,0:T(8,128)S(1)} %copy-done.19), kind=kOutput, calls=%fused_computation | convolution fusion | flops 101711872 | bytes 557056 | tf_op jit(solution)/shard_map/lpm,slp->slm/dot_general | solution.py:144
  (78 shorter events, 5.6 us)
Async XLA Ops:
  6.5 10.3 %copy-start = (f32[64,64,128]{2,1,0:T(8,128)S(1)}, f32[64,64,128]{2,1,0:T(8,128)}, u32[]{:S(2)}) copy-start(f32[64,64,128]{2,1,0:T(8,128)} %param.14) | copy-start | bytes 6291460
  6.5 5.5 %copy-start.18 = (s32[64,128]{1,0:T(8,128)S(1)}, s32[64,128]{1,0:T(8,128)}, u32[]{:S(2)}) copy-start(s32[64,128]{1,0:T(8,128)} %param.13) | copy-start | bytes 98308
  6.5 53.5 %all-gather.2.cloned.1.call-start = ((), (), s32[]{:S(2)}) async-start(), calls=%async_computation.1 | async-start | bytes 1310720 | tf_op jit(solution)/shard_map/all_gather | solution.py:72
  6.5 5.5 %copy-start.17 = (f32[8,8192]{1,0:T(8,128)S(1)}, f32[8,8192]{1,0:T(8,128)}, u32[]{:S(2)}) copy-start(f32[8,8192]{1,0:T(8,128)} %param.10) | copy-start | bytes 786436
  9.1 12.3 %copy-start.1 = (f32[16,64,128]{2,1,0:T(8,128)}, f32[16,64,128]{2,1,0:T(8,128)S(1)}, u32[]{:S(2)}) copy-start(f32[16,64,128]{2,1,0:T(8,128)S(1)} %slice_bitcast_fusion.1) | copy-start | bytes 1572868
  11.2 11.3 %copy-start.4 = (f32[4,64,128]{2,1,0:T(8,128)}, f32[4,64,128]{2,1,0:T(8,128)S(1)}, u32[]{:S(2)}) copy-start(f32[4,64,128]{2,1,0:T(8,128)S(1)} %slice_bitcast_fusion.3) | copy-start | bytes 393220
  12.1 10.7 %copy-start.7 = (f32[2,64,128]{2,1,0:T(8,128)}, f32[2,64,128]{2,1,0:T(8,128)S(1)}, u32[]{:S(2)}) copy-start(f32[2,64,128]{2,1,0:T(8,128)S(1)} %slice_bitcast_fusion.4) | copy-start | bytes 196612
  16.9 5.2 %copy-start.5 = (f32[64,128,8]{1,2,0:T(8,128)}, f32[64,128,8]{1,2,0:T(8,128)S(1)}, u32[]{:S(2)}) copy-start(f32[64,128,8]{1,2,0:T(8,128)S(1)} %fusion.2) | copy-start | bytes 786436
  21.4 1.4 %copy-start.6 = (f32[16,8,64]{2,1,0:T(8,128)}, f32[16,8,64]{2,1,0:T(8,128)S(1)}, u32[]{:S(2)}) copy-start(f32[16,8,64]{2,1,0:T(8,128)S(1)} %bitcast_reduce_fusion.1) | copy-start | bytes 98308
  22.1 1.6 %copy-start.11 = (f32[8,8,64]{2,1,0:T(8,128)}, f32[8,8,64]{2,1,0:T(8,128)S(1)}, u32[]{:S(2)}) copy-start(f32[8,8,64]{2,1,0:T(8,128)S(1)} %bitcast_reduce_fusion.2) | copy-start | bytes 49156
  22.8 6.7 %copy-start.12 = (f32[2,8,64]{2,1,0:T(8,128)}, f32[2,8,64]{2,1,0:T(8,128)S(1)}, u32[]{:S(2)}) copy-start(f32[2,8,64]{2,1,0:T(8,128)S(1)} %bitcast_reduce_fusion.4) | copy-start | bytes 12292
  23.7 30.9 %collective-permute-start.2 = (f32[8,64]{1,0:T(8,128)}, f32[8,64]{1,0:T(8,128)}, u32[]{:S(2)}, u32[]{:S(2)}) collective-permute-start(f32[8,64]{1,0:T(8,128)} %fusion.12), channel_id=1, source_target_pairs={{0,4},{4,0},{8,12},{12,8},{16,20},{20,16},{24,28},{28,24},{1,5},{5... | collective-permute-start | bytes 6152 | tf_op jit(solution)/shard_map/ppermute | solution.py:36
  27.4 0.6 copy-start.9
  29.5 8.8 %collective-permute-start.3 = (f32[8,64]{1,0:T(8,128)}, f32[8,64]{1,0:T(8,128)}, u32[]{:S(2)}, u32[]{:S(2)}) collective-permute-start(f32[8,64]{1,0:T(8,128)} %fusion.68), channel_id=1, source_target_pairs={{0,4},{4,0},{8,12},{12,8},{16,20},{20,16},{24,28},{28,24},{1,5},{5... | collective-permute-start | bytes 6152 | tf_op jit(solution)/shard_map/ppermute | solution.py:36
  30.2 8.1 %copy-start.20 = (f32[1,63]{1,0:T(1,128)}, f32[1,63]{1,0:T(1,128)S(1)}, u32[]{:S(2)}) copy-start(f32[1,63]{1,0:T(1,128)S(1)} %convert_element_type.18) | copy-start | bytes 760
  30.4 7.9 %copy-start.13 = (f32[2,8,64]{2,1,0:T(8,128)S(1)}, f32[2,8,64]{2,1,0:T(8,128)}, u32[]{:S(2)}) copy-start(f32[2,8,64]{2,1,0:T(8,128)} %copy-done.12) | copy-start | bytes 12292
  30.4 16.2 %copy-start.16 = (s32[64,4]{0,1:T(4,128)S(1)}, s32[64,4]{0,1:T(4,128)}, u32[]{:S(2)}) copy-start(s32[64,4]{0,1:T(4,128)} %param.12) | copy-start | bytes 3076
  30.4 17.5 %copy-start.15 = (s32[6]{0:T(128)S(1)}, s32[6]{0:T(128)}, u32[]{:S(2)}) copy-start(s32[6]{0:T(128)} %param.19) | copy-start | bytes 76
  32.1 9.9 %copy-start.8 = (f32[2,64,128]{2,1,0:T(8,128)S(1)}, f32[2,64,128]{2,1,0:T(8,128)}, u32[]{:S(2)}) copy-start(f32[2,64,128]{2,1,0:T(8,128)} %copy-done.7) | copy-start | bytes 196612
  32.1 22.2 %copy-start.10 = (f32[64,128]{1,0:T(8,128)S(1)}, f32[64,128]{1,0:T(8,128)}, u32[]{:S(2)}) copy-start(f32[64,128]{1,0:T(8,128)} %copy-done.9) | copy-start | bytes 98308
  34.5 22.7 %copy-start.14 = (f32[4,8,64]{2,1,0:T(8,128)S(1)}, f32[4,8,64]{2,1,0:T(8,128)}, u32[]{:S(2)}) copy-start(f32[4,8,64]{2,1,0:T(8,128)} %convolution_multiply_fusion.3) | copy-start | bytes 24580
  39.9 3.7 %collective-permute-start.5 = (f32[8,64]{1,0:T(8,128)S(1)}, f32[8,64]{1,0:T(8,128)S(1)}, u32[]{:S(2)}, u32[]{:S(2)}) collective-permute-start(f32[8,64]{1,0:T(8,128)S(1)} %fusion.55), channel_id=1, source_target_pairs={{0,8},{8,0},{4,12},{12,4},{16,24},{24,16},{20,28},{28,20},{1,9},{9... | collective-permute-start | bytes 6152 | tf_op jit(solution)/shard_map/ppermute | solution.py:36
  43.6 7.8 %collective-permute-start.6 = (f32[8,64]{1,0:T(8,128)S(1)}, f32[8,64]{1,0:T(8,128)S(1)}, u32[]{:S(2)}, u32[]{:S(2)}) collective-permute-start(f32[8,64]{1,0:T(8,128)S(1)} %add_multiply_fusion), channel_id=1, source_target_pairs={{0,16},{16,0},{4,20},{20,4},{8,24},{24,8},{12,28},{28,12},{1,17},{... | collective-permute-start | bytes 6152 | tf_op jit(solution)/shard_map/ppermute | solution.py:36
  49.8 3.7 %collective-permute-start.4 = (f32[8,64]{1,0:T(8,128)S(1)}, f32[8,64]{1,0:T(8,128)S(1)}, u32[]{:S(2)}, u32[]{:S(2)}) collective-permute-start(f32[8,64]{1,0:T(8,128)S(1)} %add_multiply_fusion.1), channel_id=1, source_target_pairs={{0,8},{8,0},{4,12},{12,4},{16,24},{24,16},{20,28},{28,20},{1,9},{9... | collective-permute-start | bytes 6152 | tf_op jit(solution)/shard_map/ppermute | solution.py:36
  60.0 11.4 %copy-start.3 = (f32[32,8192]{1,0:T(8,128)S(1)}, f32[32,8192]{1,0:T(8,128)}, u32[]{:S(2)}) copy-start(f32[32,8192]{1,0:T(8,128)} %all-gather.2.cloned.1.call-done) | copy-start | bytes 3145732
  61.1 7.3 %collective-permute-start = (f32[32,1024]{1,0:T(8,128)S(1)}, f32[32,1024]{1,0:T(8,128)S(1)}, u32[]{:S(2)}, u32[]{:S(2)}) collective-permute-start(f32[32,1024]{1,0:T(8,128)S(1)} %get-tuple-element.5), channel_id=1, source_target_pairs={{0,4},{4,8},{8,12},{12,16},{16,20},{20,24},{24,28},{1,5},{5,9},{9,... | collective-permute-start | bytes 393224 | tf_op jit(solution)/shard_map/ppermute | solution.py:20
  64.5 6.9 %collective-permute-start.1 = (f32[32,1024]{1,0:T(8,128)S(1)}, f32[32,1024]{1,0:T(8,128)S(1)}, u32[]{:S(2)}, u32[]{:S(2)}) collective-permute-start(f32[32,1024]{1,0:T(8,128)S(1)} %get-tuple-element.6), channel_id=1, source_target_pairs={{4,0},{8,4},{12,8},{16,12},{20,16},{24,20},{28,24},{5,1},{9,5},{13... | collective-permute-start | bytes 393224 | tf_op jit(solution)/shard_map/ppermute | solution.py:22
  71.7 2.2 %copy-start.2 = (f32[64,4,32,128]{3,2,1,0:T(8,128)S(1)}, f32[64,4,32,128]{3,2,1,0:T(8,128)}, u32[]{:S(2)}) copy-start(f32[64,4,32,128]{3,2,1,0:T(8,128)} %param.11) | copy-start | bytes 12582916
  83.6 9.4 %all-to-all-start = ((f32[4,1,16384]{2,1,0:T(1,128)}), f32[4,1,16384]{2,1,0:T(1,128)S(1)}, u32[]{:S(2)}, u32[]{:S(2)}) async-start(f32[4,1,16384]{2,1,0:T(1,128)} %reshape.130), calls=%async_computation | async-start | bytes 524288 | tf_op jit(solution)/shard_map/all_to_all | solution.py:78
  95.2 2.1 %copy-start.19 = (s32[64,128]{1,0:T(8,128)S(1)}, s32[64,128]{1,0:T(8,128)}, u32[]{:S(2)}) copy-start(s32[64,128]{1,0:T(8,128)} %param.13) | copy-start | bytes 98308
Sparse Core Ops, SparseCore 0:
  29.6 18.5 all-gather.1
where the time goes:
time: 109 us; the launch traced here: 108 us
  matrix products  47.1 us (43%)
  starting transfers between devices  18.3 us (17%)
  local copies, waits for them, and re-layouts  15.3 us (14%)
  between operations  15 us (14%)
  waiting for transfers between devices  7.65 us (7%)
  other arithmetic  4.46 us (4%)
    ppermute x5, starting transfers between devices, partner(): return lax.ppermute(block, axis, route)  9.76 us
    dot_general x5, matrix products, local(): jnp.einsum('jkm,jsm->jsk', transfer, spread, precision=precise)  9.07 us
    dot_general x5, matrix products, local(): jnp.einsum('jkm,jsm->jsk', blocks[:, :, :skel_rank], sibling, precision=p...  6.3 us
    dot_general x1, matrix products, near_product(): return jnp.einsum('lnqp,slnp->slq', tile_rows, sources, precision=precise)  6.21 us
    slice x5, local copies, waits for them, and re-layouts, local(): blocks = local_blocks[first_node:first_node + node_count]  5.5 us
    dot_general x1, matrix products, local(): jnp.einsum('lpm,slm->slp', order_hot, panels.reshape(rhs_dev, leaves, lea...  4.75 us
    all_to_all x1, starting transfers between devices, local(): lax.all_to_all(partial_rows, 'vec', split_axis=0, concat_axis=2, tiled=True)  3.63 us
    unnamed x45, local copies, waits for them, and re-layouts  3.58 us
  transfers between devices with their start and end apart: 9, of which 5 were waited for; matrix products, arithmetic and copies ran while one was open for 26% of the time, Pallas kernels for 0%

commit v1 on v0

--- a/solution.py
+++ b/solution.py
@@ -75,7 +75,12 @@
     partial_rows = near_product(
         near_tiles, jnp.einsum("lne,sep->slnp", select_hot, blocked, precision=precise)
     )
-    near_field = lax.all_to_all(partial_rows, "vec", split_axis=0, concat_axis=2, tiled=True)
+    near_field = jnp.concatenate(
+        lax.all_to_all(
+            jnp.stack(jnp.split(partial_rows, lax.axis_size("vec"), axis=0)), "vec", 0, 0
+        ),
+        axis=2,
+    )
     local_blocks = local_mats[0]
     local_admit = local_flags[0].astype(jnp.float32)
     leaf_skel = jnp.einsum("lkp,slp->lsk", leaf_basis, ordered, precision=precise)

time: 109 us -> 109 us (level)
    transpose x1 -> x0, local copies, waits for them, and re-layouts: 1.39 us -> none  [near_product(): return jnp.einsum('lnqp,slnp->slq', tile_rows, sources, precision=precise)]
    another operation x1 -> x3, local copies, waits for them, and re-layouts: 0.01 us -> 1.23 us  [the longest x2 1.22 us: local(): jnp.stack(jnp.split(partial_rows, lax.axis_size('vec'), axis=0))]
where the time goes in v1:
time: 109 us; the launch traced here: 108 us
  matrix products  47.2 us (43%)
  starting transfers between devices  18.3 us (17%)
  local copies, waits for them, and re-layouts  15.1 us (14%)
  between operations  15 us (14%)
  waiting for transfers between devices  7.64 us (7%)
  other arithmetic  4.53 us (4%)
    ppermute x5, starting transfers between devices, partner(): return lax.ppermute(block, axis, route)  9.76 us
    dot_general x5, matrix products, local(): jnp.einsum('jkm,jsm->jsk', transfer, spread, precision=precise)  9.07 us
    dot_general x5, matrix products, local(): jnp.einsum('jkm,jsm->jsk', blocks[:, :, :skel_rank], sibling, precision=p...  6.31 us
    dot_general x1, matrix products, near_product(): return jnp.einsum('lnqp,slnp->slq', tile_rows, sources, precision=precise)  6.25 us
    slice x5, local copies, waits for them, and re-layouts, local(): blocks = local_blocks[first_node:first_node + node_count]  5.5 us
    dot_general x1, matrix products, local(): jnp.einsum('lpm,slm->slp', order_hot, panels.reshape(rhs_dev, leaves, lea...  4.75 us
    all_to_all x1, starting transfers between devices, local(): lax.all_to_all(jnp.stack(jnp.split(partial_rows, lax.axis_size('vec'), ax...  3.63 us
    unnamed x45, local copies, waits for them, and re-layouts  3.58 us
  transfers between devices with their start and end apart: 9, of which 5 were waited for; matrix products, arithmetic and copies ran while one was open for 26% of the time, Pallas kernels for 0%

profile of v1, /device:TPU:0, one launch (start us, length us, event | category | flops | bytes accessed | tf_op | source)
XLA Modules:
  0.0 107.8 jit_solution(13122835773621150606)
XLA Ops:
  6.5 1.4 %slice_bitcast_fusion = f32[32,64,128]{2,1,0:T(8,128)S(1)} fusion(f32[1,63,64,128]{3,2,1,0:T(8,128)} %param.15), kind=kLoop, calls=%fused_computation.35 | loop fusion | bytes 2097152 | tf_op jit(solution)/shard_map/slice | solution.py:93
  8.0 1.1 %slice_bitcast_fusion.1 = f32[16,64,128]{2,1,0:T(8,128)S(1)} fusion(f32[1,63,64,128]{3,2,1,0:T(8,128)} %param.15), kind=kLoop, calls=%fused_computation.40 | loop fusion | bytes 1048576 | tf_op jit(solution)/shard_map/slice | solution.py:93
  9.1 1.2 %slice_bitcast_fusion.6 = f32[8,64,128]{2,1,0:T(8,128)S(1)} fusion(f32[1,63,64,128]{3,2,1,0:T(8,128)} %param.15), kind=kLoop, calls=%fused_computation.53 | loop fusion | bytes 524288 | tf_op jit(solution)/shard_map/slice | solution.py:93
  10.3 0.9 slice_bitcast_fusion.7
  11.2 0.9 slice_bitcast_fusion.8
  12.1 4.7 %fusion.2 = f32[64,128,8]{1,2,0:T(8,128)S(1)} fusion(s32[64,128]{1,0:T(8,128)S(1)} %copy-done.18, f32[8,8192]{1,0:T(8,128)S(1)} %copy-done.17), kind=kOutput, calls=%fused_computation.4 | convolution fusion | flops 101711872 | bytes 557056 | tf_op jit(solution)/shard_map/lpm,slm->slp/dot_general | solution.py:65
  16.9 3.4 %bitcast_reduce_fusion = f32[32,8,64]{2,1,0:T(8,128)S(1)} fusion(f32[64,64,128]{2,1,0:T(8,128)S(1)} %copy-done, f32[64,128,8]{1,2,0:T(8,128)S(1)} %fusion.2), kind=kOutput, calls=%fused_computation.49 | convolution fusion | flops 50348032 | bytes 2424832 | tf_op jit(solution)/shard_map/lkp,slp->lsk/dot_general | solution.py:86
  20.2 1.2 %bitcast_reduce_fusion.1 = f32[16,8,64]{2,1,0:T(8,128)S(1)} fusion(f32[32,64,128]{2,1,0:T(8,128)S(1)} %slice_bitcast_fusion, f32[32,8,64]{2,1,0:T(8,128)S(1)} %bitcast_reduce_fusion), kind=kOutput, calls=%fused_computation.58 | convolution fusion | flops 12607488 | bytes 1146880 | tf_op jit(solution)/shard_map/jsk,jkm->jsm/dot_general | solution.py:99
  21.4 0.7 bitcast_reduce_fusion.2
  22.8 0.8 fusion.12
  23.7 3.0 %collective-permute-start.2 = (f32[8,64]{1,0:T(8,128)}, f32[8,64]{1,0:T(8,128)}, u32[]{:S(2)}, u32[]{:S(2)}) collective-permute-start(f32[8,64]{1,0:T(8,128)} %fusion.12), channel_id=1, source_target_pairs={{0,4},{4,0},{8,12},{12,8},{16,20},{20,16},{24,28},{28,24},{1,5},{5... | collective-permute-start | bytes 6152 | tf_op jit(solution)/shard_map/ppermute | solution.py:36
  26.6 0.8 slice_bitcast_fusion.9
  28.0 1.5 %fusion.68 = f32[8,64]{1,0:T(8,128)} fusion(f32[8,64]{1,0:T(8,128)} %fusion.12, f32[64,128]{1,0:T(8,128)S(1)} %slice_bitcast_fusion.9), kind=kOutput, calls=%fused_computation.89 | convolution fusion | flops 393216 | bytes 36864 | tf_op jit(solution)/shard_map/dot_general | solution.py:103
  29.5 0.7 convert_element_type.18
  30.5 0.8 reverse_multiply_fusion.2
  31.2 0.8 reverse_multiply_fusion.1
  32.1 1.9 %convolution_multiply_fusion.3 = f32[4,8,64]{2,1,0:T(8,128)} fusion(f32[4,8,64]{2,1,0:T(8,128)S(1)} %bitcast.154, f32[4,64,128]{2,1,0:T(8,128)} %copy-done.4, f32[4]{0:T(128)S(1)} %slice_bitcast_fusion.11), kind=kOutput, calls=%fused_computation.20 | convolution fusion | flops 1574912 | bytes 147472 | tf_op jit(solution)/shard_map/jkm,jsm->jsk/dot_general | solution.py:97
  34.5 2.0 %convolution_multiply_fusion.1 = f32[16,8,64]{2,1,0:T(8,128)S(1)} fusion(f32[16,8,64]{2,1,0:T(8,128)S(1)} %bitcast.149, f32[16,64,128]{2,1,0:T(8,128)} %copy-done.1, f32[16]{0:T(128)S(1)} %slice_bitcast_fusion.13), kind=kOutput, calls=%fused_computation.16 | convolution fusion | flops 6299648 | bytes 589888 | tf_op jit(solution)/shard_map/jkm,jsm->jsk/dot_general | solution.py:97
  36.5 1.8 %convolution_multiply_fusion = f32[32,8,64]{2,1,0:T(8,128)S(1)} fusion(f32[32,8,64]{2,1,0:T(8,128)S(1)} %bitcast.146, f32[32,64,128]{2,1,0:T(8,128)S(1)} %slice_bitcast_fusion, f32[32]{0:T(128)S(1)} %slice_bitcast_fusion.14), kind=kOutput, calls=%fused_computation.14 | convolution fusion | flops 12599296 | bytes 1179776 | tf_op jit(solution)/shard_map/jkm,jsm->jsk/dot_general | solution.py:97
  38.3 0.7 add_multiply_fusion.1
  39.0 0.9 fusion.55
  39.9 2.1 %collective-permute-start.5 = (f32[8,64]{1,0:T(8,128)S(1)}, f32[8,64]{1,0:T(8,128)S(1)}, u32[]{:S(2)}, u32[]{:S(2)}) collective-permute-start(f32[8,64]{1,0:T(8,128)S(1)} %fusion.55), channel_id=1, source_target_pairs={{0,8},{8,0},{4,12},{12,4},{16,24},{24,16},{20,28},{28,20},{1,9},{9... | collective-permute-start | bytes 6152 | tf_op jit(solution)/shard_map/ppermute | solution.py:36
  42.2 1.4 %collective-permute-done.5 = f32[8,64]{1,0:T(8,128)S(1)} collective-permute-done((f32[8,64]{1,0:T(8,128)S(1)}, f32[8,64]{1,0:T(8,128)S(1)}, u32[]{:S(2)}, u32[]{:S(2)}) %collective-permute-start.5) | collective-permute-done | bytes 2080 | tf_op jit(solution)/shard_map/ppermute | solution.py:36
  43.6 3.0 %collective-permute-start.6 = (f32[8,64]{1,0:T(8,128)S(1)}, f32[8,64]{1,0:T(8,128)S(1)}, u32[]{:S(2)}, u32[]{:S(2)}) collective-permute-start(f32[8,64]{1,0:T(8,128)S(1)} %add_multiply_fusion), channel_id=1, source_target_pairs={{0,16},{16,0},{4,20},{20,4},{8,24},{24,8},{12,28},{28,12},{1,17},{... | collective-permute-start | bytes 6152 | tf_op jit(solution)/shard_map/ppermute | solution.py:36
  46.7 1.3 %slice.157 = f32[1,1]{1,0:T(1,128)} slice(f32[1,63]{1,0:T(1,128)} %copy-done.20), slice={[0:1], [62:63]} | slice | bytes 8 | tf_op jit(solution)/shard_map/slice | solution.py:119
  49.8 1.6 %collective-permute-start.4 = (f32[8,64]{1,0:T(8,128)S(1)}, f32[8,64]{1,0:T(8,128)S(1)}, u32[]{:S(2)}, u32[]{:S(2)}) collective-permute-start(f32[8,64]{1,0:T(8,128)S(1)} %add_multiply_fusion.1), channel_id=1, source_target_pairs={{0,8},{8,0},{4,12},{12,4},{16,24},{24,16},{20,28},{28,20},{1,9},{9... | collective-permute-start | bytes 6152 | tf_op jit(solution)/shard_map/ppermute | solution.py:36
  51.4 0.9 convolution_multiply_fusion.5
  52.3 0.9 fusion.53
  53.4 0.9 fusion.10
  54.6 1.5 %fusion.11 = f32[8,64]{1,0:T(8,128)S(1)} fusion(f32[8,64]{1,0:T(8,128)S(1)} %fusion.66, f32[8,64]{1,0:T(8,128)} %collective-permute-done.2, f32[64,128]{1,0:T(8,128)S(1)} %copy-done.10, f32[]{:T(128)} %bitcast.39), kind=kOutput, calls=%fused_computation.27 | convolution fusion | flops 394240 | bytes 38916 | tf_op jit(solution)/shard_map/dot_general | solution.py:126
  56.1 1.1 %convolution_add_fusion.4 = f32[2,8,64]{2,1,0:T(8,128)S(1)} fusion(f32[2,8,64]{2,1,0:T(8,128)S(1)} %convolution_multiply_fusion.4, f32[63,64,128]{2,1,0:T(8,128)} %bitcast.134, f32[8,64]{1,0:T(8,128)S(1)} %fusion.11), kind=kOutput, calls=%fused_computation.21 | convolution fusion | flops 787456 | bytes 75776 | tf_op jit(solution)/shard_map/jkm,jsm->jsk/dot_general | solution.py:142
  57.2 1.3 %convolution_add_fusion.3 = f32[4,8,64]{2,1,0:T(8,128)S(1)} fusion(f32[4,8,64]{2,1,0:T(8,128)S(1)} %copy-done.14, f32[4,8,64]{2,1,0:T(8,128)S(1)} %bitcast.155, f32[63,64,128]{2,1,0:T(8,128)} %bitcast.135), kind=kOutput, calls=%fused_computation.19 | convolution fusion | flops 1574912 | bytes 155648 | tf_op jit(solution)/shard_map/jkm,jsm->jsk/dot_general | solution.py:142
  58.5 1.5 %convolution_add_fusion.2 = f32[8,8,64]{2,1,0:T(8,128)S(1)} fusion(f32[8,8,64]{2,1,0:T(8,128)S(1)} %convolution_multiply_fusion.2, f32[8,8,64]{2,1,0:T(8,128)S(1)} %bitcast.153, f32[63,64,128]{2,1,0:T(8,128)} %bitcast.136), kind=kOutput, calls=%fused_computation.17 | convolution fusion | flops 3149824 | bytes 311296 | tf_op jit(solution)/shard_map/jkm,jsm->jsk/dot_general | solution.py:142
  60.1 1.1 fusion.94
  61.2 3.4 %collective-permute-start = (f32[32,1024]{1,0:T(8,128)S(1)}, f32[32,1024]{1,0:T(8,128)S(1)}, u32[]{:S(2)}, u32[]{:S(2)}) collective-permute-start(f32[32,1024]{1,0:T(8,128)S(1)} %get-tuple-element.9), channel_id=1, source_target_pairs={{0,4},{4,8},{8,12},{12,16},{16,20},{20,24},{24,28},{1,5},{5,9},{9,... | collective-permute-start | bytes 393224 | tf_op jit(solution)/shard_map/ppermute | solution.py:20
  64.6 1.5 %collective-permute-start.1 = (f32[32,1024]{1,0:T(8,128)S(1)}, f32[32,1024]{1,0:T(8,128)S(1)}, u32[]{:S(2)}, u32[]{:S(2)}) collective-permute-start(f32[32,1024]{1,0:T(8,128)S(1)} %get-tuple-element.10), channel_id=1, source_target_pairs={{4,0},{8,4},{12,8},{16,12},{20,16},{24,20},{28,24},{5,1},{9,5},{13... | collective-permute-start | bytes 393224 | tf_op jit(solution)/shard_map/ppermute | solution.py:22
  66.1 2.0 %convolution_add_fusion.1 = f32[16,8,64]{2,1,0:T(8,128)S(1)} fusion(f32[16,8,64]{2,1,0:T(8,128)S(1)} %convolution_multiply_fusion.1, f32[16,8,64]{2,1,0:T(8,128)S(1)} %bitcast.150, f32[63,64,128]{2,1,0:T(8,128)} %bitcast.137), kind=kOutput, calls=%fused_computation.15 | convolution fusion | flops 6299648 | bytes 622592 | tf_op jit(solution)/shard_map/jkm,jsm->jsk/dot_general | solution.py:142
  68.5 3.0 %collective-permute-done.1 = f32[32,1024]{1,0:T(8,128)S(1)} collective-permute-done((f32[32,1024]{1,0:T(8,128)S(1)}, f32[32,1024]{1,0:T(8,128)S(1)}, u32[]{:S(2)}, u32[]{:S(2)}) %collective-permute-start.1) | collective-permute-done | bytes 131104 | tf_op jit(solution)/shard_map/ppermute | solution.py:22
  71.8 1.9 %convolution_bitcast_fusion.1 = f32[32,64,4,128]{3,1,2,0:T(8,128)S(1)} fusion(f32[32,80,128,1]{2,1,0,3:T(8,128)S(1)} %bitcast.139, s32[64,4]{0,1:T(4,128)S(1)} %subtract_add_fusion), kind=kOutput, calls=%fused_computation.5 | convolution fusion | flops 1006653440 | bytes 5506048 | tf_op jit(solution)/shard_map/lne,sep->slnp/dot_general | solution.py:76
  74.0 6.2 %fusion.5 = f32[32,64,32]{2,0,1:T(8,128)S(1)} fusion(f32[64,4,32,128]{3,2,1,0:T(8,128)S(1)} %copy-done.2, f32[32,64,4,128]{3,1,2,0:T(8,128)S(1)} %convolution_bitcast_fusion.1), kind=kOutput, calls=%fused_computation.8 | convolution fusion | flops 402653184 | bytes 8650752 | tf_op jit(solution)/shard_map/lnqp,slnp->slq/dot_general | solution.py:40
  80.4 1.2 %copy.16 = f32[4,8,64,32]{2,3,1,0:T(8,128)} copy(f32[4,8,64,32]{3,1,2,0:T(8,128)S(1)} %pad_maximum_fusion) | data formatting | bytes 524288 | tf_op jit(solution)/shard_map/stack | solution.py:80
  81.5 2.1 %reshape.138 = f32[4,1,16384]{2,1,0:T(1,128)} reshape(f32[4,8,32,64]{3,2,1,0:T(8,128)} %bitcast.140) | data formatting | bytes 524288
  83.6 3.6 %all-to-all-start = ((f32[4,1,16384]{2,1,0:T(1,128)}), f32[4,1,16384]{2,1,0:T(1,128)S(1)}, u32[]{:S(2)}, u32[]{:S(2)}) async-start(f32[4,1,16384]{2,1,0:T(1,128)} %reshape.138), calls=%async_computation | async-start | bytes 524288 | tf_op jit(solution)/shard_map/all_to_all | solution.py:79
  87.3 3.0 %convolution_add_fusion = f32[32,8,64]{2,1,0:T(8,128)S(1)} fusion(f32[32,8,64]{2,1,0:T(8,128)S(1)} %convolution_multiply_fusion, f32[32,8,64]{2,1,0:T(8,128)S(1)} %bitcast.147, f32[63,64,128]{2,1,0:T(8,128)} %bitcast.138), kind=kOutput, calls=%fused_computation.13 | convolution fusion | flops 12599296 | bytes 1245184 | tf_op jit(solution)/shard_map/jkm,jsm->jsk/dot_general | solution.py:142
  90.3 2.7 %all-to-all-done = f32[4,1,16384]{2,1,0:T(1,128)S(1)} async-done(((f32[4,1,16384]{2,1,0:T(1,128)}), f32[4,1,16384]{2,1,0:T(1,128)S(1)}, u32[]{:S(2)}, u32[]{:S(2)}) %all-to-all-start) | async-done | bytes 262176 | tf_op jit(solution)/shard_map/all_to_all | solution.py:79
  93.5 1.4 %reduce.2 = f32[4,16384]{1,0:T(4,128)S(1)} reduce(f32[4,1,16384]{2,1,0:T(1,128)S(1)} %all-to-all-done, f32[]{:T(128)} %broadcast.17), dimensions={1}, to_apply=%all_to_all.3.reduce_sub_computation | reduce | bytes 524292 | tf_op jit(solution)/shard_map/all_to_all | solution.py:79
  95.5 1.9 %fusion.9 = f32[8,64,128]{2,0,1:T(8,128)S(1)} fusion(f32[8,64,128]{2,0,1:T(8,128)S(1)} %copy.18, f32[64,8,64]{2,1,0:T(8,128)S(1)} %bitcast.144, f32[64,64,128]{2,1,0:T(8,128)S(1)} %copy-done), kind=kOutput, calls=%fused_computation.12 | convolution fusion | flops 50397184 | bytes 2752512 | tf_op jit(solution)/shard_map/lkp,lsk->slp/dot_general | solution.py:145
  97.4 3.6 %convolution_bitcast_fusion = f32[8,8192]{1,0:T(8,128)} fusion(f32[8,64,128]{2,0,1:T(8,128)S(1)} %fusion.9, s32[64,128]{1,0:T(8,128)S(1)} %copy-done.19), kind=kOutput, calls=%fused_computation | convolution fusion | flops 101711872 | bytes 557056 | tf_op jit(solution)/shard_map/lpm,slp->slm/dot_general | solution.py:149
  (81 shorter events, 5.7 us)
Async XLA Ops:
  6.5 10.3 %copy-start = (f32[64,64,128]{2,1,0:T(8,128)S(1)}, f32[64,64,128]{2,1,0:T(8,128)}, u32[]{:S(2)}) copy-start(f32[64,64,128]{2,1,0:T(8,128)} %param.14) | copy-start | bytes 6291460
  6.5 5.5 %copy-start.18 = (s32[64,128]{1,0:T(8,128)S(1)}, s32[64,128]{1,0:T(8,128)}, u32[]{:S(2)}) copy-start(s32[64,128]{1,0:T(8,128)} %param.13) | copy-start | bytes 98308
  6.5 53.5 %all-gather.2.cloned.1.call-start = ((), (), s32[]{:S(2)}) async-start(), calls=%async_computation.1 | async-start | bytes 1310720 | tf_op jit(solution)/shard_map/all_gather | solution.py:72
  6.5 5.5 %copy-start.17 = (f32[8,8192]{1,0:T(8,128)S(1)}, f32[8,8192]{1,0:T(8,128)}, u32[]{:S(2)}) copy-start(f32[8,8192]{1,0:T(8,128)} %param.10) | copy-start | bytes 786436
  9.1 12.3 %copy-start.1 = (f32[16,64,128]{2,1,0:T(8,128)}, f32[16,64,128]{2,1,0:T(8,128)S(1)}, u32[]{:S(2)}) copy-start(f32[16,64,128]{2,1,0:T(8,128)S(1)} %slice_bitcast_fusion.1) | copy-start | bytes 1572868
  11.2 11.3 %copy-start.4 = (f32[4,64,128]{2,1,0:T(8,128)}, f32[4,64,128]{2,1,0:T(8,128)S(1)}, u32[]{:S(2)}) copy-start(f32[4,64,128]{2,1,0:T(8,128)S(1)} %slice_bitcast_fusion.7) | copy-start | bytes 393220
  12.1 10.7 %copy-start.7 = (f32[2,64,128]{2,1,0:T(8,128)}, f32[2,64,128]{2,1,0:T(8,128)S(1)}, u32[]{:S(2)}) copy-start(f32[2,64,128]{2,1,0:T(8,128)S(1)} %slice_bitcast_fusion.8) | copy-start | bytes 196612
  16.9 5.2 %copy-start.5 = (f32[64,128,8]{1,2,0:T(8,128)}, f32[64,128,8]{1,2,0:T(8,128)S(1)}, u32[]{:S(2)}) copy-start(f32[64,128,8]{1,2,0:T(8,128)S(1)} %fusion.2) | copy-start | bytes 786436
  21.4 1.4 %copy-start.6 = (f32[16,8,64]{2,1,0:T(8,128)}, f32[16,8,64]{2,1,0:T(8,128)S(1)}, u32[]{:S(2)}) copy-start(f32[16,8,64]{2,1,0:T(8,128)S(1)} %bitcast_reduce_fusion.1) | copy-start | bytes 98308
  22.1 1.6 %copy-start.11 = (f32[8,8,64]{2,1,0:T(8,128)}, f32[8,8,64]{2,1,0:T(8,128)S(1)}, u32[]{:S(2)}) copy-start(f32[8,8,64]{2,1,0:T(8,128)S(1)} %bitcast_reduce_fusion.2) | copy-start | bytes 49156
  22.8 6.7 %copy-start.12 = (f32[2,8,64]{2,1,0:T(8,128)}, f32[2,8,64]{2,1,0:T(8,128)S(1)}, u32[]{:S(2)}) copy-start(f32[2,8,64]{2,1,0:T(8,128)S(1)} %bitcast_reduce_fusion.4) | copy-start | bytes 12292
  23.7 30.9 %collective-permute-start.2 = (f32[8,64]{1,0:T(8,128)}, f32[8,64]{1,0:T(8,128)}, u32[]{:S(2)}, u32[]{:S(2)}) collective-permute-start(f32[8,64]{1,0:T(8,128)} %fusion.12), channel_id=1, source_target_pairs={{0,4},{4,0},{8,12},{12,8},{16,20},{20,16},{24,28},{28,24},{1,5},{5... | collective-permute-start | bytes 6152 | tf_op jit(solution)/shard_map/ppermute | solution.py:36
  27.4 0.6 copy-start.9
  29.5 8.8 %collective-permute-start.3 = (f32[8,64]{1,0:T(8,128)}, f32[8,64]{1,0:T(8,128)}, u32[]{:S(2)}, u32[]{:S(2)}) collective-permute-start(f32[8,64]{1,0:T(8,128)} %fusion.68), channel_id=1, source_target_pairs={{0,4},{4,0},{8,12},{12,8},{16,20},{20,16},{24,28},{28,24},{1,5},{5... | collective-permute-start | bytes 6152 | tf_op jit(solution)/shard_map/ppermute | solution.py:36
  30.2 8.1 %copy-start.20 = (f32[1,63]{1,0:T(1,128)}, f32[1,63]{1,0:T(1,128)S(1)}, u32[]{:S(2)}) copy-start(f32[1,63]{1,0:T(1,128)S(1)} %convert_element_type.18) | copy-start | bytes 760
  30.4 7.9 %copy-start.13 = (f32[2,8,64]{2,1,0:T(8,128)S(1)}, f32[2,8,64]{2,1,0:T(8,128)}, u32[]{:S(2)}) copy-start(f32[2,8,64]{2,1,0:T(8,128)} %copy-done.12) | copy-start | bytes 12292
  30.4 16.2 %copy-start.16 = (s32[64,4]{0,1:T(4,128)S(1)}, s32[64,4]{0,1:T(4,128)}, u32[]{:S(2)}) copy-start(s32[64,4]{0,1:T(4,128)} %param.12) | copy-start | bytes 3076
  30.4 17.5 %copy-start.15 = (s32[6]{0:T(128)S(1)}, s32[6]{0:T(128)}, u32[]{:S(2)}) copy-start(s32[6]{0:T(128)} %param.19) | copy-start | bytes 76
  32.1 9.9 %copy-start.8 = (f32[2,64,128]{2,1,0:T(8,128)S(1)}, f32[2,64,128]{2,1,0:T(8,128)}, u32[]{:S(2)}) copy-start(f32[2,64,128]{2,1,0:T(8,128)} %copy-done.7) | copy-start | bytes 196612
  32.1 22.2 %copy-start.10 = (f32[64,128]{1,0:T(8,128)S(1)}, f32[64,128]{1,0:T(8,128)}, u32[]{:S(2)}) copy-start(f32[64,128]{1,0:T(8,128)} %copy-done.9) | copy-start | bytes 98308
  34.5 22.7 %copy-start.14 = (f32[4,8,64]{2,1,0:T(8,128)S(1)}, f32[4,8,64]{2,1,0:T(8,128)}, u32[]{:S(2)}) copy-start(f32[4,8,64]{2,1,0:T(8,128)} %convolution_multiply_fusion.3) | copy-start | bytes 24580
  39.9 3.7 %collective-permute-start.5 = (f32[8,64]{1,0:T(8,128)S(1)}, f32[8,64]{1,0:T(8,128)S(1)}, u32[]{:S(2)}, u32[]{:S(2)}) collective-permute-start(f32[8,64]{1,0:T(8,128)S(1)} %fusion.55), channel_id=1, source_target_pairs={{0,8},{8,0},{4,12},{12,4},{16,24},{24,16},{20,28},{28,20},{1,9},{9... | collective-permute-start | bytes 6152 | tf_op jit(solution)/shard_map/ppermute | solution.py:36
  43.6 7.8 %collective-permute-start.6 = (f32[8,64]{1,0:T(8,128)S(1)}, f32[8,64]{1,0:T(8,128)S(1)}, u32[]{:S(2)}, u32[]{:S(2)}) collective-permute-start(f32[8,64]{1,0:T(8,128)S(1)} %add_multiply_fusion), channel_id=1, source_target_pairs={{0,16},{16,0},{4,20},{20,4},{8,24},{24,8},{12,28},{28,12},{1,17},{... | collective-permute-start | bytes 6152 | tf_op jit(solution)/shard_map/ppermute | solution.py:36
  49.8 3.7 %collective-permute-start.4 = (f32[8,64]{1,0:T(8,128)S(1)}, f32[8,64]{1,0:T(8,128)S(1)}, u32[]{:S(2)}, u32[]{:S(2)}) collective-permute-start(f32[8,64]{1,0:T(8,128)S(1)} %add_multiply_fusion.1), channel_id=1, source_target_pairs={{0,8},{8,0},{4,12},{12,4},{16,24},{24,16},{20,28},{28,20},{1,9},{9... | collective-permute-start | bytes 6152 | tf_op jit(solution)/shard_map/ppermute | solution.py:36
  60.1 11.4 %copy-start.3 = (f32[32,8192]{1,0:T(8,128)S(1)}, f32[32,8192]{1,0:T(8,128)}, u32[]{:S(2)}) copy-start(f32[32,8192]{1,0:T(8,128)} %all-gather.2.cloned.1.call-done) | copy-start | bytes 3145732
  61.2 7.3 %collective-permute-start = (f32[32,1024]{1,0:T(8,128)S(1)}, f32[32,1024]{1,0:T(8,128)S(1)}, u32[]{:S(2)}, u32[]{:S(2)}) collective-permute-start(f32[32,1024]{1,0:T(8,128)S(1)} %get-tuple-element.9), channel_id=1, source_target_pairs={{0,4},{4,8},{8,12},{12,16},{16,20},{20,24},{24,28},{1,5},{5,9},{9,... | collective-permute-start | bytes 393224 | tf_op jit(solution)/shard_map/ppermute | solution.py:20
  64.6 6.9 %collective-permute-start.1 = (f32[32,1024]{1,0:T(8,128)S(1)}, f32[32,1024]{1,0:T(8,128)S(1)}, u32[]{:S(2)}, u32[]{:S(2)}) collective-permute-start(f32[32,1024]{1,0:T(8,128)S(1)} %get-tuple-element.10), channel_id=1, source_target_pairs={{4,0},{8,4},{12,8},{16,12},{20,16},{24,20},{28,24},{5,1},{9,5},{13... | collective-permute-start | bytes 393224 | tf_op jit(solution)/shard_map/ppermute | solution.py:22
  71.8 2.2 %copy-start.2 = (f32[64,4,32,128]{3,2,1,0:T(8,128)S(1)}, f32[64,4,32,128]{3,2,1,0:T(8,128)}, u32[]{:S(2)}) copy-start(f32[64,4,32,128]{3,2,1,0:T(8,128)} %param.11) | copy-start | bytes 12582916
  83.6 9.4 %all-to-all-start = ((f32[4,1,16384]{2,1,0:T(1,128)}), f32[4,1,16384]{2,1,0:T(1,128)S(1)}, u32[]{:S(2)}, u32[]{:S(2)}) async-start(f32[4,1,16384]{2,1,0:T(1,128)} %reshape.138), calls=%async_computation | async-start | bytes 524288 | tf_op jit(solution)/shard_map/all_to_all | solution.py:79
  95.3 2.1 %copy-start.19 = (s32[64,128]{1,0:T(8,128)S(1)}, s32[64,128]{1,0:T(8,128)}, u32[]{:S(2)}) copy-start(s32[64,128]{1,0:T(8,128)} %param.13) | copy-start | bytes 98308
Sparse Core Ops, SparseCore 0:
  29.7 18.5 all-gather.1
